TPU v7x, 256 devices: a whole 4x4x8 slice. The times are simulated.
256 devices in a mesh: edge: 64 (over y, z, core), pix: 4 (over x).
Axes of the slice: x: 4, y: 4, z: 8, core: 2. Of those that a mesh axis runs over, the one named last changes fastest.
Arguments:
- features: bfloat16 [128, 48, 64, 128], P('edge', 'pix'), may hold values from -6 to 6
- poses: float32 [128, 6], replicated, may hold values from -1.5 to 1.5
- inv_depth: float32 [128, 3072], P('edge', 'pix'), may hold values from 0.25 to 2
- hidden: bfloat16 [256, 48, 64, 128], P('edge', 'pix'), may hold values from -1 to 1
- edges: int32 [256, 2], P('edge'), may hold values from 0 to 127, as said below
- counts: int32 [64], P('edge'), may hold values from 1 to 4, 128 in all
- w_gates: bfloat16 [9, 256, 256], replicated, may hold values from -0.125 to 0.125
- w_cand: bfloat16 [9, 256, 128], replicated, may hold values from -0.125 to 0.125
- w_head: bfloat16 [4, 128], replicated, may hold values from -0.5 to 0.5
Outputs:
- hidden_out: bfloat16 [256, 48, 64, 128], P('edge', 'pix')
- pose_update: float32 [128, 6], P('edge')
- depth_update: float32 [128, 3072], P('edge', 'pix')
Inputs may be any that keep to these rules, and one draw needn't show every extreme that they name: `edges`: slot s lies on node n = s // 4; its source frame is 2n or 2n + 1 and its target is one of the frames 2n to 2n + 3 other than the source; on the last node the target is the other frame of its own pair. The first slot of node n goes from frame 2n to frame 2n + 2 (on the last node to 2n + 1). Dead slots hold such pairs too.
All inputs are finite; a program needn't handle non-finite values. No bound on the sum of `counts` on one device may be relied on, other than what follows from the above.
Results may differ from a plain program's by a relative error of at most 0.011.
Values may be sent and summed in bfloat16 or wider, within the bound.
No kernel may reach another device: no remote copies, remote signals or barrier semaphores. Data moves between devices by JAX's collectives and lax.ppermute only.
A program may use at most 192 MiB of HBM per device.

v0:
```python
import math
import jax
import jax.numpy as jnp
from jax import lax
from jax.sharding import PartitionSpec as P

PRECISE = lax.Precision.HIGHEST
POSE_DAMPING = 0.1
DEPTH_DAMPING = 0.1


def passed_along(value, axis, steps):
    count = lax.axis_size(axis)
    first, last = (max(0, -steps), min(count, count - steps))
    return lax.ppermute(value, axis, [(source, source + steps) for source in range(first, last)])


def padded_2(cells, sides, width):
    for axis, dim in sides:
        count = lax.axis_size(axis)
        ends = count - 1
        head = lax.slice_in_dim(cells, 0, width, axis=dim)
        tail = lax.slice_in_dim(cells, cells.shape[dim] - width, cells.shape[dim], axis=dim)
        cells = jnp.concatenate(
            [
                lax.ppermute(tail, axis, [(i, (i + 1) % count) for i in range(ends)]),
                cells,
                lax.ppermute(head, axis, [((i + 1) % count, i) for i in range(ends)]),
            ],
            axis=dim,
        )
    return cells


def pixel_coords(row_start, row_count, total_rows, col_count):
    row_ids = (row_start + lax.broadcasted_iota(jnp.int32, (row_count, col_count), 0)).astype(
        jnp.float32
    )
    col_ids = lax.broadcasted_iota(jnp.int32, (row_count, col_count), 1).astype(jnp.float32)
    half_width = col_count / 2.0
    horizontal = (col_ids - (col_count - 1) / 2.0) / half_width
    vertical = (row_ids - (total_rows - 1) / 2.0) / half_width
    return (horizontal.reshape(-1), vertical.reshape(-1))


def match_rows(queries, targets, factor):
    scores = jnp.einsum("pc,qc->pq", queries, targets, preferred_element_type=jnp.float32) * factor
    row_max = jnp.max(scores, axis=1, keepdims=True)
    weights = jnp.exp(scores - row_max)
    row_total = jnp.sum(weights, axis=1, keepdims=True)
    weighted_sum = jnp.dot(
        weights.astype(jnp.bfloat16), targets, preferred_element_type=jnp.float32
    )
    return (weighted_sum / row_total).astype(jnp.bfloat16)


def conv_taps(framed, weight, row_count, col_count):
    padded = jnp.pad(framed, ((0, 0), (0, 0), (1, 1), (0, 0)))
    result = None
    for tap_index in range(9):
        row_off = tap_index // 3
        col_off = tap_index % 3
        window = padded[:, row_off : row_off + row_count, col_off : col_off + col_count, :]
        tap_term = jnp.einsum(
            "srwc,cd->srwd", window, weight[tap_index], preferred_element_type=jnp.float32
        )
        result = tap_term if tap_index == 0 else result + tap_term
    return result


def bundle_terms(head_out, live_mask, inv_rho, xi_rel, src_local, tgt_local, horizontal, vertical):
    flow_pred = head_out[:, 0:2]
    confidence = jax.nn.sigmoid(head_out[:, 2:4]) * live_mask[:, None, None]
    unit_row = jnp.ones_like(inv_rho)
    zero_row = jnp.zeros_like(inv_rho)
    horiz_row = horizontal[None, :] * unit_row
    vert_row = vertical[None, :] * unit_row
    jacobian_horiz = jnp.stack(
        [
            inv_rho,
            zero_row,
            -horiz_row * inv_rho,
            -horiz_row * vert_row,
            1.0 + horiz_row * horiz_row,
            -vert_row,
        ],
        axis=1,
    )
    jacobian_vert = jnp.stack(
        [
            zero_row,
            inv_rho,
            -vert_row * inv_rho,
            -(1.0 + vert_row * vert_row),
            horiz_row * vert_row,
            horiz_row,
        ],
        axis=1,
    )
    jacobian = jnp.stack([jacobian_horiz, jacobian_vert], axis=1)
    predicted = jnp.einsum("skjp,sj->skp", jacobian, xi_rel, precision=PRECISE)
    residual = flow_pred - predicted
    forward_shift = xi_rel[:, 2:3]
    depth_jacobian = jnp.stack(
        [xi_rel[:, 0:1] - horiz_row * forward_shift, xi_rel[:, 1:2] - vert_row * forward_shift],
        axis=1,
    )
    frame_ids = jnp.arange(4, dtype=jnp.int32)
    select = (tgt_local[:, None] == frame_ids[None, :]).astype(jnp.float32) - (
        src_local[:, None] == frame_ids[None, :]
    ).astype(jnp.float32)
    slot_count, pix_count = inv_rho.shape
    pose_jacobian = (select[:, None, :, None, None] * jacobian[:, :, None, :, :]).reshape(
        slot_count, 2, 24, pix_count
    )
    weighted = pose_jacobian * confidence[:, :, None, :]
    pose_pose = jnp.einsum("skip,skjp->ij", weighted, pose_jacobian, precision=PRECISE)
    pose_rhs = jnp.einsum("skip,skp->i", weighted, residual, precision=PRECISE)
    pose_depth_slot = jnp.einsum("skip,skp->sip", weighted, depth_jacobian, precision=PRECISE)
    depth_depth_slot = jnp.sum(confidence * depth_jacobian * depth_jacobian, axis=1)
    depth_rhs_slot = jnp.sum(confidence * depth_jacobian * residual, axis=1)
    source_pick = (src_local[:, None] == frame_ids[None, 0:2]).astype(jnp.float32)
    pose_depth = jnp.einsum("sf,sip->fip", source_pick, pose_depth_slot, precision=PRECISE)
    depth_depth = DEPTH_DAMPING + jnp.einsum(
        "sf,sp->fp", source_pick, depth_depth_slot, precision=PRECISE
    )
    depth_rhs = jnp.einsum("sf,sp->fp", source_pick, depth_rhs_slot, precision=PRECISE)
    depth_ratio = pose_depth / depth_depth[:, None, :]
    reduced = pose_pose - jnp.einsum("fip,fjp->ij", depth_ratio, pose_depth, precision=PRECISE)
    reduced_rhs = pose_rhs - jnp.einsum("fip,fp->i", depth_ratio, depth_rhs, precision=PRECISE)
    return (reduced, reduced_rhs, pose_depth, depth_depth, depth_rhs)


def factor_solve(factor_low, rhs_mat):
    lower_part = lax.linalg.triangular_solve(factor_low, rhs_mat, left_side=True, lower=True)
    return lax.linalg.triangular_solve(
        factor_low, lower_part, left_side=True, lower=True, transpose_a=True
    )


def sweep_nodes(blocks, vectors):
    node_total = blocks.shape[0]
    node_ids = jnp.arange(node_total, dtype=jnp.int32)
    same_node = (node_ids[:, None] == node_ids[None, :]).astype(jnp.float32)
    next_node = (node_ids[None, :] == node_ids[:, None] + 1).astype(jnp.float32)
    previous_far = jnp.concatenate(
        [jnp.zeros((1, 12, 12), jnp.float32), blocks[:-1, 12:, 12:]], axis=0
    )
    diag_blocks = blocks[:, :12, :12] + previous_far
    link_blocks = blocks[:, :12, 12:]
    dense = jnp.einsum("nm,nij->nimj", same_node, diag_blocks, precision=PRECISE)
    upper = jnp.einsum("nm,nij->nimj", next_node, link_blocks, precision=PRECISE)
    dense = dense + upper + jnp.transpose(upper, (2, 3, 0, 1))
    system_size = 12 * node_total
    system = dense.reshape(system_size, system_size) + POSE_DAMPING * jnp.eye(
        system_size, dtype=jnp.float32
    )
    previous_rhs = jnp.concatenate([jnp.zeros((1, 12), jnp.float32), vectors[:-1, 12:]], axis=0)
    system_rhs = (vectors[:, :12] + previous_rhs).reshape(system_size)
    factor_low = jnp.linalg.cholesky(system)
    solution = factor_solve(factor_low, system_rhs[:, None])[:, 0]
    return solution.reshape(node_total, 12)


def shards(features, poses, inv_depth, hidden, edges, counts, w_gates, w_cand, w_head):
    slot_count, row_count, col_count, hid_width = hidden.shape
    channels = features.shape[3]
    frame_count = poses.shape[0]
    node_rank = lax.axis_index("edge")
    base_frame = 2 * node_rank
    pix_rank = lax.axis_index("pix")
    total_rows = row_count * lax.axis_size("pix")
    local_pixels = row_count * col_count
    own_whole = lax.all_gather(features, "pix", axis=1, tiled=True)
    next_whole = passed_along(own_whole, "edge", -1)
    nearby = jnp.concatenate([own_whole, next_whole], axis=0)
    nearby = nearby.reshape(4, total_rows * col_count, channels)
    own_flat = features.reshape(2, local_pixels, channels)
    src_local = edges[:, 0] - base_frame
    tgt_local = edges[:, 1] - base_frame
    factor = 2.0 / math.sqrt(channels)
    matched_list = []
    for slot_index in range(slot_count):
        queries = lax.dynamic_index_in_dim(own_flat, src_local[slot_index], 0, keepdims=False)
        targets = lax.dynamic_index_in_dim(nearby, tgt_local[slot_index], 0, keepdims=False)
        matched_list.append(match_rows(queries, targets, factor))
    matched = jnp.stack(matched_list, axis=0).reshape(slot_count, row_count, col_count, channels)
    inputs = jnp.concatenate([hidden, matched], axis=3)
    state_wide = hidden.astype(jnp.float32)
    framed = padded_2(inputs, (("pix", 1),), 1)
    gates = jax.nn.sigmoid(conv_taps(framed, w_gates, row_count, col_count))
    update = gates[..., :hid_width]
    reset_state = (gates[..., hid_width:] * state_wide).astype(jnp.bfloat16)
    reset_framed = padded_2(reset_state, (("pix", 1),), 1)
    second = jnp.concatenate([reset_framed, framed[..., hid_width:]], axis=3)
    candidate = jnp.tanh(conv_taps(second, w_cand, row_count, col_count))
    fresh = ((1.0 - update) * state_wide + update * candidate).astype(jnp.bfloat16)
    live_mask = (lax.broadcasted_iota(jnp.int32, (slot_count,), 0) < counts[0]).astype(jnp.float32)
    hidden_out = jnp.where(live_mask[:, None, None, None] > 0.5, fresh, hidden)
    head_out = jnp.einsum(
        "kc,spc->skp",
        w_head,
        fresh.reshape(slot_count, local_pixels, hid_width),
        preferred_element_type=jnp.float32,
    )
    pair_ids = jnp.arange(2, dtype=jnp.int32)
    source_pick = (src_local[:, None] == pair_ids[None, :]).astype(jnp.float32)
    inv_rho = jnp.dot(source_pick, inv_depth, precision=PRECISE)
    all_ids = jnp.arange(frame_count, dtype=jnp.int32)
    frame_diff = (edges[:, 1:2] == all_ids[None, :]).astype(jnp.float32) - (
        edges[:, 0:1] == all_ids[None, :]
    ).astype(jnp.float32)
    xi_rel = jnp.dot(frame_diff, poses, precision=PRECISE)
    horizontal, vertical = pixel_coords(pix_rank * row_count, row_count, total_rows, col_count)
    reduced_part, rhs_part, pose_depth, depth_depth, depth_rhs = bundle_terms(
        head_out, live_mask, inv_rho, xi_rel, src_local, tgt_local, horizontal, vertical
    )
    reduced, reduced_rhs = lax.psum((reduced_part, rhs_part), "pix")
    blocks, vectors = (
        lax.all_gather(reduced[None], "edge", axis=0, tiled=True),
        lax.all_gather(reduced_rhs[None], "edge", axis=0, tiled=True),
    )
    values = sweep_nodes(blocks, vectors)
    node_total = values.shape[0]
    node_pose = lax.dynamic_index_in_dim(values, node_rank, 0, keepdims=False)
    after_index = jnp.minimum(node_rank + 1, node_total - 1)
    next_pose = lax.dynamic_index_in_dim(values, after_index, 0, keepdims=False) * (
        node_rank + 1 < node_total
    ).astype(jnp.float32)
    pose_update = node_pose.reshape(2, 6)
    pose_pair = jnp.concatenate([node_pose, next_pose], axis=0)
    depth_update = (
        depth_rhs - jnp.einsum("fip,i->fp", pose_depth, pose_pair, precision=PRECISE)
    ) / depth_depth
    return (hidden_out, pose_update, depth_update)


def solution(mesh):
    placed = (
        P("edge", "pix", None, None),
        P(),
        P("edge", "pix"),
        P("edge", "pix", None, None),
        P("edge", None),
        P("edge"),
        P(),
        P(),
        P(),
    )
    return jax.shard_map(
        shards,
        mesh=mesh,
        in_specs=placed,
        out_specs=(P("edge", "pix", None, None), P("edge", None), P("edge", "pix")),
        check_vma=False,
    )
```

profile of v0, /device:TPU:1, one launch (start us, length us, event | category | flops | bytes accessed | tf_op | source)
XLA Modules:
  0.0 581.9 jit_solution(17546545287537749910)
XLA Ops:
  22.5 20.2 %all-gather.3.cloned.1.call-done = bf16[2,48,64,128]{3,2,1,0:T(8,128)(2,1)} async-done(((bf16[2,12,64,128]{3,2,1,0:T(8,128)(2,1)}), bf16[2,48,64,128]{3,2,1,0:T(8,128)(2,1)}) %all-gather.3.cloned.1.call-update) | async-done | bytes 1572880 | tf_op jit(solution)/shard_map/all_gather | solution.py:174
  51.2 13.6 %collective-permute-done = bf16[2,48,64,128]{3,2,1,0:T(8,128)(2,1)S(1)} collective-permute-done((bf16[2,48,64,128]{3,2,1,0:T(8,128)(2,1)}, bf16[2,48,64,128]{3,2,1,0:T(8,128)(2,1)S(1)}, u32[]{:S(2)}, u32[]{:S(2)}) %collective-permute-start) | collective-permute-done | bytes 1572896 | tf_op jit(solution)/shard_map/ppermute | solution.py:15
  103.2 4.9 add_divide_fusion
  109.7 4.4 collective-permute-start.3
  126.7 13.3 %all-reduce.5 = (f32[1,24,24]{2,1,0:T(8,128)S(1)}, f32[1,24]{1,0:T(1,128)S(1)}) all-reduce(f32[1,24,24]{2,1,0:T(8,128)S(1)} %fusion.97, f32[1,24]{1,0:T(1,128)S(1)} %fusion.106), channel_id=1, replica_groups=mesh['edge'=64,'pix'=4] {'pix'}, use_global_device_ids=true, to_apply=%region_9.10 | all-reduce | flops 600 | bytes 4800 | tf_op jit(solution)/shard_map/psum | solution.py:218
  139.9 58.5 %all_gather.10 = f32[64,24,24]{2,1,0:T(8,128)S(1)} all-gather(f32[1,24,24]{2,1,0:T(8,128)S(1)} %get-tuple-element.36), channel_id=1, replica_groups=mesh['edge'=64,'pix'=4] {'edge'}, dimensions={0}, use_global_device_ids=true | all-gather | bytes 149760 | tf_op jit(solution)/shard_map/all_gather | solution.py:220
  200.0 12.3 %fusion = f32[64,12,64,12]{1,0,3,2:T(8,128)} fusion(f32[64,64]{0,1:T(8,128)S(1)} %get-tuple-element.125, f32[64,12,12]{1,0,2:T(8,128)S(1)} %copy.62, f32[64,64]{0,1:T(8,128)S(1)} %get-tuple-element.124, f32[64,12,12]{1,0,2:T(8,128)S(1)} %copy.61), kind=kLoop, calls=%fused_computation.4 | loop fusion | flops 1769472 | bytes 2465792 | tf_op jit(solution)/shard_map/add | solution.py:153
  212.3 33.5 %copy.63 = f32[64,12,64,12]{3,2,1,0:T(8,128)} copy(f32[64,12,64,12]{1,0,3,2:T(8,128)} %fusion) | data formatting | bytes 4718592 | tf_op jit(solution)/shard_map/add | solution.py:153
  245.9 18.1 %fusion.1 = f32[64,12,64,12]{3,2,1,0:T(8,128)} fusion(f32[64,12,64,12]{3,2,1,0:T(8,128)} %copy.63, f32[64,64]{0,1:T(8,128)S(1)} %get-tuple-element.125, f32[64,12,12]{1,0,2:T(8,128)S(1)} %copy.62), kind=kLoop, calls=%fused_computation.5 | loop fusion | flops 1179648 | bytes 4771840 | tf_op jit(solution)/shard_map/add | solution.py:153
  264.0 22.7 %reshape.435 = f32[768,768]{1,0:T(8,128)} reshape(f32[64,12,64,12]{3,2,1,0:T(8,128)} %fusion.1) | data formatting | bytes 4718592 | tf_op jit(solution)/shard_map/reshape | solution.py:155
  297.0 11.7 %cholesky.164 = f32[128,128]{1,0:T(8,128)S(1)} custom-call(f32[128,128]{1,0:T(8,128)S(1)} %cholesky.421), custom_call_target="Cholesky" | custom-call | tf_op jit(solution)/shard_map/jit(cholesky)/cholesky | solution.py:160
  308.9 9.8 %custom-call.48 = f32[1,128,128]{1,2,0:T(8,128)S(1)} custom-call(f32[1,128,128]{2,1,0:T(8,128)S(1)} %get-tuple-element.60), custom_call_target="InvertDiagBlocksLowerTriangular" | custom-call | tf_op jit(solution)/shard_map/jit(cholesky)/cholesky | solution.py:160
  321.7 11.7 %cholesky.187 = f32[128,128]{1,0:T(8,128)S(1)} custom-call(f32[128,128]{1,0:T(8,128)S(1)} %cholesky.425), custom_call_target="Cholesky" | custom-call | tf_op jit(solution)/shard_map/jit(cholesky)/cholesky | solution.py:160
  333.5 10.2 %custom-call.49 = f32[1,128,128]{1,2,0:T(8,128)S(1)} custom-call(f32[1,128,128]{2,1,0:T(8,128)S(1)} %get-tuple-element.58), custom_call_target="InvertDiagBlocksLowerTriangular" | custom-call | tf_op jit(solution)/shard_map/jit(cholesky)/cholesky | solution.py:160
  346.3 11.7 %cholesky.352 = f32[128,128]{1,0:T(8,128)S(1)} custom-call(f32[128,128]{1,0:T(8,128)S(1)} %cholesky.430), custom_call_target="Cholesky" | custom-call | tf_op jit(solution)/shard_map/jit(cholesky)/cholesky | solution.py:160
  358.2 9.8 %custom-call.50 = f32[1,128,128]{1,2,0:T(8,128)S(1)} custom-call(f32[1,128,128]{2,1,0:T(8,128)S(1)} %get-tuple-element.56), custom_call_target="InvertDiagBlocksLowerTriangular" | custom-call | tf_op jit(solution)/shard_map/jit(cholesky)/cholesky | solution.py:160
  370.5 11.9 %cholesky.371 = f32[128,128]{1,0:T(8,128)S(1)} custom-call(f32[128,128]{1,0:T(8,128)S(1)} %cholesky.435), custom_call_target="Cholesky" | custom-call | tf_op jit(solution)/shard_map/jit(cholesky)/cholesky | solution.py:160
  382.6 9.8 %custom-call.51 = f32[1,128,128]{1,2,0:T(8,128)S(1)} custom-call(f32[1,128,128]{2,1,0:T(8,128)S(1)} %get-tuple-element.54), custom_call_target="InvertDiagBlocksLowerTriangular" | custom-call | tf_op jit(solution)/shard_map/jit(cholesky)/cholesky | solution.py:160
  394.6 11.7 %cholesky.390 = f32[128,128]{1,0:T(8,128)S(1)} custom-call(f32[128,128]{1,0:T(8,128)S(1)} %cholesky.440), custom_call_target="Cholesky" | custom-call | tf_op jit(solution)/shard_map/jit(cholesky)/cholesky | solution.py:160
  406.5 9.8 %custom-call.52 = f32[1,128,128]{1,2,0:T(8,128)S(1)} custom-call(f32[1,128,128]{2,1,0:T(8,128)S(1)} %get-tuple-element.52), custom_call_target="InvertDiagBlocksLowerTriangular" | custom-call | tf_op jit(solution)/shard_map/jit(cholesky)/cholesky | solution.py:160
  418.4 11.7 %cholesky.408 = f32[128,128]{1,0:T(8,128)S(1)} custom-call(f32[128,128]{1,0:T(8,128)S(1)} %convolution_subtract_fusion.4), custom_call_target="Cholesky" | custom-call | tf_op jit(solution)/shard_map/jit(cholesky)/cholesky | solution.py:160
  434.2 37.7 %all-gather = f32[64,1,24]{2,1,0:T(1,128)S(1)} all-gather(f32[1,1,24]{2,1,0:T(1,128)S(1)} %bitcast.562), channel_id=1, replica_groups=mesh['edge'=64,'pix'=4] {'edge'}, dimensions={0}, use_global_device_ids=true | all-gather | bytes 6240 | tf_op jit(solution)/shard_map/all_gather | solution.py:221
  477.5 21.6 %while.1 = (s32[]{:T(128)}, f32[768,768]{0,1:T(8,128)}, s32[6,2]{0,1:T(2,128)S(1)}, f32[6,128,128]{2,1,0:T(8,128)}, s32[]{:T(128)}) while((s32[]{:T(128)}, f32[768,768]{0,1:T(8,128)}, s32[6,2]{0,1:T(2,128)S(1)}, f32[6,128,128]{2,1,0:T(8,128)}, s32[]{:T(128)}) %tuple.82), condition=%wide.while_cond, body=%wide.while_body.sunk | while | flops 2 | bytes 393329 | solution.py:136
  499.1 59.8 %custom-call.53 = f32[6,128,128]{1,2,0:T(8,128)S(1)} custom-call(f32[6,128,128]{2,1,0:T(8,128)} %get-tuple-element.10), custom_call_target="InvertDiagBlocksLowerTriangular" | custom-call | tf_op jit(solution)/shard_map/triangular_solve | solution.py:136
  (231 shorter events, 128.4 us)
Async XLA Ops:
  7.2 15.0 %copy-start = (f32[2,768]{1,0:T(2,128)S(1)}, f32[2,768]{1,0:T(2,128)}, u32[]{:S(2)}) copy-start(f32[2,768]{1,0:T(2,128)} %param.11) | copy-start | bytes 18436
  7.2 35.5 %all-gather.3.cloned.1.call-start = ((), (), s32[]{:S(2)}) async-start(), calls=%async_computation | async-start | bytes 1966080 | tf_op jit(solution)/shard_map/all_gather | solution.py:174
  42.7 22.0 %collective-permute-start = (bf16[2,48,64,128]{3,2,1,0:T(8,128)(2,1)}, bf16[2,48,64,128]{3,2,1,0:T(8,128)(2,1)S(1)}, u32[]{:S(2)}, u32[]{:S(2)}) collective-permute-start(bf16[2,48,64,128]{3,2,1,0:T(8,128)(2,1)} %all-gather.3.cloned.1.call-done), channel_id=1, source_target_pairs={{4,0},{8,4},{12,8},{16,12},{20,16},{24,20},{28,24},{32,28},{36,32}... | collective-permute-start | bytes 4718600 | tf_op jit(solution)/shard_map/ppermute | solution.py:15
  51.2 15.3 %copy-start.4 = (bf16[2,12,64,128]{3,2,1,0:T(8,128)(2,1)S(1)}, bf16[2,12,64,128]{3,2,1,0:T(8,128)(2,1)}, u32[]{:S(2)}) copy-start(bf16[2,12,64,128]{3,2,1,0:T(8,128)(2,1)} %param.9) | copy-start | bytes 1179652
  85.7 2.1 copy-start.2
  85.7 7.5 %copy-start.5 = (bf16[9,256,256]{2,1,0:T(8,128)(2,1)S(1)}, bf16[9,256,256]{2,1,0:T(8,128)(2,1)}, u32[]{:S(2)}) copy-start(bf16[9,256,256]{2,1,0:T(8,128)(2,1)} %param.15) | copy-start | bytes 3538948
  87.9 7.6 %collective-permute-start.2 = (bf16[4,1,64,256]{3,2,1,0:T(8,128)(2,1)S(1)}, bf16[4,1,64,256]{3,2,1,0:T(8,128)(2,1)S(1)}, u32[]{:S(2)}, u32[]{:S(2)}) collective-permute-start(bf16[4,1,64,256]{3,2,1,0:T(8,128)(2,1)S(1)} %get-tuple-element.45), channel_id=1, source_target_pairs={{1,0},{2,1},{3,2},{5,4},{6,5},{7,6},{9,8},{10,9},{11,10},{13,12},{... | collective-permute-start | bytes 393224 | tf_op jit(solution)/shard_map/ppermute | solution.py:28
  89.2 6.3 %collective-permute-start.1 = (bf16[4,1,64,256]{3,2,1,0:T(8,128)(2,1)S(1)}, bf16[4,1,64,256]{3,2,1,0:T(8,128)(2,1)S(1)}, u32[]{:S(2)}, u32[]{:S(2)}) collective-permute-start(bf16[4,1,64,256]{3,2,1,0:T(8,128)(2,1)S(1)} %get-tuple-element.44), channel_id=1, source_target_pairs={{0,1},{1,2},{2,3},{4,5},{5,6},{6,7},{8,9},{9,10},{10,11},{12,13},{... | collective-permute-start | bytes 393224 | tf_op jit(solution)/shard_map/ppermute | solution.py:26
  108.4 6.0 %collective-permute-start.4 = (bf16[4,1,64,128]{3,2,1,0:T(8,128)(2,1)S(1)}, bf16[4,1,64,128]{3,2,1,0:T(8,128)(2,1)S(1)}, u32[]{:S(2)}, u32[]{:S(2)}) collective-permute-start(bf16[4,1,64,128]{3,2,1,0:T(8,128)(2,1)S(1)} %get-tuple-element.49), channel_id=1, source_target_pairs={{1,0},{2,1},{3,2},{5,4},{6,5},{7,6},{9,8},{10,9},{11,10},{13,12},{... | collective-permute-start | bytes 196616 | tf_op jit(solution)/shard_map/ppermute | solution.py:28
  109.7 5.4 collective-permute-start.3
  114.2 1.2 copy-start.6
  120.0 2.3 copy-start.7
  295.6 1.4 copy-start.3
  477.5 97.4 %copy-start.1 = (f32[2,768]{1,0:T(2,128)S(1)}, f32[2,768]{1,0:T(2,128)}, u32[]{:S(2)}) copy-start(f32[2,768]{1,0:T(2,128)} %param.11) | copy-start | bytes 18436
Sparse Core Ops, SparseCore 0:
  9.8 32.8 all-gather.2
where the time goes:
time: 588 us; the launch traced here: 582 us
  other arithmetic  232 us (39%)
  blocking collectives  109 us (19%)
  local copies, waits for them, and re-layouts  89.6 us (15%)
  matrix products  66.9 us (11%)
  waiting for transfers between devices  35.2 us (6%)
  between operations  34.7 us (6%)
  starting transfers between devices  13.6 us (2%)
    another operation x23, other arithmetic, sweep_nodes(): factor_low = jnp.linalg.cholesky(system)  124 us
    another operation x4, other arithmetic, factor_solve(): lax.linalg.triangular_solve(factor_low, lower_part, left_side=True, lower...  61.4 us
    all_gather x1, blocking collectives, shards(): lax.all_gather(reduced[None], 'edge', axis=0, tiled=True)  58.5 us
    all_gather x1, blocking collectives, shards(): lax.all_gather(reduced_rhs[None], 'edge', axis=0, tiled=True)  37.7 us
    add x1, local copies, waits for them, and re-layouts, sweep_nodes(): dense = dense + upper + jnp.transpose(upper, (2, 3, 0, 1))  33.5 us
    add x2, other arithmetic, sweep_nodes(): dense = dense + upper + jnp.transpose(upper, (2, 3, 0, 1))  30.4 us
    reshape x2, local copies, waits for them, and re-layouts, sweep_nodes(): dense.reshape(system_size, system_size)  24.7 us
    another operation x30, local copies, waits for them, and re-layouts  21.5 us
  transfers between devices with their start and end apart: 6, of which 3 were waited for; matrix products, arithmetic and copies ran while one was open for 1% of the time, Pallas kernels for 0%

commit v1 on v0

--- a/solution.py
+++ b/solution.py
@@ -7,6 +7,14 @@
 PRECISE = lax.Precision.HIGHEST
 POSE_DAMPING = 0.1
 DEPTH_DAMPING = 0.1
+
+
+def gather_by_exchange(array, axis, dim):
+    count = lax.axis_size(axis)
+    repeats = [count if d == dim else 1 for d in range(array.ndim)]
+    return lax.all_to_all(
+        jnp.tile(array, repeats), axis, split_axis=dim, concat_axis=dim, tiled=True
+    )
 
 
 def passed_along(value, axis, steps):
@@ -218,7 +226,7 @@
     reduced, reduced_rhs = lax.psum((reduced_part, rhs_part), "pix")
     blocks, vectors = (
         lax.all_gather(reduced[None], "edge", axis=0, tiled=True),
-        lax.all_gather(reduced_rhs[None], "edge", axis=0, tiled=True),
+        gather_by_exchange(reduced_rhs[None], "edge", 0),
     )
     values = sweep_nodes(blocks, vectors)
     node_total = values.shape[0]

time: 588 us -> 558 us (0.949)
  blocking collectives: 109 us -> 71.8 us
  starting transfers between devices: 13.6 us -> 20.2 us
    all_gather x1 -> x0, blocking collectives: 37.7 us -> none  [shards(): lax.all_gather(reduced_rhs[None], 'edge', axis=0, tiled=True)]
    all_to_all x0 -> x1, starting transfers between devices: none -> 6.54 us  [gather_by_exchange(): lax.all_to_all(jnp.tile(array, repeats), axis, split_axis=dim, concat_axi...]
    another operation x30 -> x31, local copies, waits for them, and re-layouts: 21.5 us -> 22.1 us
  transfers between devices with their start and end apart: 6 -> 7, of which waited for: 3 -> 3; matrix products, arithmetic and copies ran while one was open for 1% -> 16% of each run, Pallas kernels for 0% -> 0%
where the time goes in v1:
time: 558 us; the launch traced here: 551 us
  other arithmetic  232 us (42%)
  local copies, waits for them, and re-layouts  90.2 us (16%)
  blocking collectives  71.8 us (13%)
  matrix products  66.9 us (12%)
  waiting for transfers between devices  35.2 us (6%)
  between operations  34.7 us (6%)
  starting transfers between devices  20.2 us (4%)
    another operation x23, other arithmetic, sweep_nodes(): factor_low = jnp.linalg.cholesky(system)  124 us
    another operation x4, other arithmetic, factor_solve(): lax.linalg.triangular_solve(factor_low, lower_part, left_side=True, lower...  61.4 us
    all_gather x1, blocking collectives, shards(): lax.all_gather(reduced[None], 'edge', axis=0, tiled=True)  58.5 us
    add x1, local copies, waits for them, and re-layouts, sweep_nodes(): dense = dense + upper + jnp.transpose(upper, (2, 3, 0, 1))  33.5 us
    add x2, other arithmetic, sweep_nodes(): dense = dense + upper + jnp.transpose(upper, (2, 3, 0, 1))  30.4 us
    reshape x2, local copies, waits for them, and re-layouts, sweep_nodes(): dense.reshape(system_size, system_size)  24.7 us
    another operation x30, local copies, waits for them, and re-layouts  21.5 us
    dot_general x18, matrix products, conv_taps(): jnp.einsum('srwc,cd->srwd', window, weight[tap_index], preferred_element_...  21.5 us
  transfers between devices with their start and end apart: 7, of which 3 were waited for; matrix products, arithmetic and copies ran while one was open for 16% of the time, Pallas kernels for 0%

profile of v1, /device:TPU:1, one launch (start us, length us, event | category | flops | bytes accessed | tf_op | source)
XLA Modules:
  0.0 551.4 jit_solution(11217302521016164991)
XLA Ops:
  22.5 20.2 %all-gather.2.cloned.1.call-done = bf16[2,48,64,128]{3,2,1,0:T(8,128)(2,1)} async-done(((bf16[2,12,64,128]{3,2,1,0:T(8,128)(2,1)}), bf16[2,48,64,128]{3,2,1,0:T(8,128)(2,1)}) %all-gather.2.cloned.1.call-update) | async-done | bytes 1572880 | tf_op jit(solution)/shard_map/all_gather | solution.py:182
  51.2 13.6 %collective-permute-done = bf16[2,48,64,128]{3,2,1,0:T(8,128)(2,1)S(1)} collective-permute-done((bf16[2,48,64,128]{3,2,1,0:T(8,128)(2,1)}, bf16[2,48,64,128]{3,2,1,0:T(8,128)(2,1)S(1)}, u32[]{:S(2)}, u32[]{:S(2)}) %collective-permute-start) | collective-permute-done | bytes 1572896 | tf_op jit(solution)/shard_map/ppermute | solution.py:23
  103.2 4.9 add_divide_fusion
  109.7 4.4 collective-permute-start.3
  126.7 13.3 %all-reduce.5 = (f32[1,24,24]{2,1,0:T(8,128)S(1)}, f32[24]{0:T(128)S(1)}) all-reduce(f32[1,24,24]{2,1,0:T(8,128)S(1)} %fusion.97, f32[24]{0:T(128)S(1)} %fusion.105), channel_id=1, replica_groups=mesh['edge'=64,'pix'=4] {'pix'}, use_global_device_ids=true, to_apply=%region_9.10 | all-reduce | flops 600 | bytes 4800 | tf_op jit(solution)/shard_map/psum | solution.py:226
  139.9 58.5 %all_gather.7 = f32[64,24,24]{2,1,0:T(8,128)S(1)} all-gather(f32[1,24,24]{2,1,0:T(8,128)S(1)} %get-tuple-element.36), channel_id=1, replica_groups=mesh['edge'=64,'pix'=4] {'edge'}, dimensions={0}, use_global_device_ids=true | all-gather | bytes 149760 | tf_op jit(solution)/shard_map/all_gather | solution.py:228
  200.0 12.3 %fusion = f32[64,12,64,12]{1,0,3,2:T(8,128)} fusion(f32[64,64]{0,1:T(8,128)S(1)} %get-tuple-element.125, f32[64,12,12]{1,0,2:T(8,128)S(1)} %copy.62, f32[64,64]{0,1:T(8,128)S(1)} %get-tuple-element.124, f32[64,12,12]{1,0,2:T(8,128)S(1)} %copy.61), kind=kLoop, calls=%fused_computation.4 | loop fusion | flops 1769472 | bytes 2465792 | tf_op jit(solution)/shard_map/add | solution.py:161
  212.3 33.5 %copy.63 = f32[64,12,64,12]{3,2,1,0:T(8,128)} copy(f32[64,12,64,12]{1,0,3,2:T(8,128)} %fusion) | data formatting | bytes 4718592 | tf_op jit(solution)/shard_map/add | solution.py:161
  245.9 18.1 %fusion.1 = f32[64,12,64,12]{3,2,1,0:T(8,128)} fusion(f32[64,12,64,12]{3,2,1,0:T(8,128)} %copy.63, f32[64,64]{0,1:T(8,128)S(1)} %get-tuple-element.125, f32[64,12,12]{1,0,2:T(8,128)S(1)} %copy.62), kind=kLoop, calls=%fused_computation.5 | loop fusion | flops 1179648 | bytes 4771840 | tf_op jit(solution)/shard_map/add | solution.py:161
  264.0 22.7 %reshape.443 = f32[768,768]{1,0:T(8,128)} reshape(f32[64,12,64,12]{3,2,1,0:T(8,128)} %fusion.1) | data formatting | bytes 4718592 | tf_op jit(solution)/shard_map/reshape | solution.py:163
  297.0 11.7 %cholesky.164 = f32[128,128]{1,0:T(8,128)S(1)} custom-call(f32[128,128]{1,0:T(8,128)S(1)} %cholesky.421), custom_call_target="Cholesky" | custom-call | tf_op jit(solution)/shard_map/jit(cholesky)/cholesky | solution.py:168
  308.9 9.8 %custom-call.48 = f32[1,128,128]{1,2,0:T(8,128)S(1)} custom-call(f32[1,128,128]{2,1,0:T(8,128)S(1)} %get-tuple-element.60), custom_call_target="InvertDiagBlocksLowerTriangular" | custom-call | tf_op jit(solution)/shard_map/jit(cholesky)/cholesky | solution.py:168
  321.7 11.7 %cholesky.187 = f32[128,128]{1,0:T(8,128)S(1)} custom-call(f32[128,128]{1,0:T(8,128)S(1)} %cholesky.425), custom_call_target="Cholesky" | custom-call | tf_op jit(solution)/shard_map/jit(cholesky)/cholesky | solution.py:168
  333.5 10.2 %custom-call.49 = f32[1,128,128]{1,2,0:T(8,128)S(1)} custom-call(f32[1,128,128]{2,1,0:T(8,128)S(1)} %get-tuple-element.58), custom_call_target="InvertDiagBlocksLowerTriangular" | custom-call | tf_op jit(solution)/shard_map/jit(cholesky)/cholesky | solution.py:168
  346.3 11.7 %cholesky.352 = f32[128,128]{1,0:T(8,128)S(1)} custom-call(f32[128,128]{1,0:T(8,128)S(1)} %cholesky.430), custom_call_target="Cholesky" | custom-call | tf_op jit(solution)/shard_map/jit(cholesky)/cholesky | solution.py:168
  358.2 9.8 %custom-call.50 = f32[1,128,128]{1,2,0:T(8,128)S(1)} custom-call(f32[1,128,128]{2,1,0:T(8,128)S(1)} %get-tuple-element.56), custom_call_target="InvertDiagBlocksLowerTriangular" | custom-call | tf_op jit(solution)/shard_map/jit(cholesky)/cholesky | solution.py:168
  370.5 11.9 %cholesky.371 = f32[128,128]{1,0:T(8,128)S(1)} custom-call(f32[128,128]{1,0:T(8,128)S(1)} %cholesky.435), custom_call_target="Cholesky" | custom-call | tf_op jit(solution)/shard_map/jit(cholesky)/cholesky | solution.py:168
  382.6 9.8 %custom-call.51 = f32[1,128,128]{1,2,0:T(8,128)S(1)} custom-call(f32[1,128,128]{2,1,0:T(8,128)S(1)} %get-tuple-element.54), custom_call_target="InvertDiagBlocksLowerTriangular" | custom-call | tf_op jit(solution)/shard_map/jit(cholesky)/cholesky | solution.py:168
  394.6 11.7 %cholesky.390 = f32[128,128]{1,0:T(8,128)S(1)} custom-call(f32[128,128]{1,0:T(8,128)S(1)} %cholesky.440), custom_call_target="Cholesky" | custom-call | tf_op jit(solution)/shard_map/jit(cholesky)/cholesky | solution.py:168
  406.5 9.8 %custom-call.52 = f32[1,128,128]{1,2,0:T(8,128)S(1)} custom-call(f32[1,128,128]{2,1,0:T(8,128)S(1)} %get-tuple-element.52), custom_call_target="InvertDiagBlocksLowerTriangular" | custom-call | tf_op jit(solution)/shard_map/jit(cholesky)/cholesky | solution.py:168
  418.4 11.7 %cholesky.408 = f32[128,128]{1,0:T(8,128)S(1)} custom-call(f32[128,128]{1,0:T(8,128)S(1)} %convolution_subtract_fusion.4), custom_call_target="Cholesky" | custom-call | tf_op jit(solution)/shard_map/jit(cholesky)/cholesky | solution.py:168
  434.8 6.5 %all-to-all-start = ((f32[64,1,24]{2,1,0:T(1,128)}), f32[64,1,24]{2,1,0:T(1,128)S(1)}, u32[]{:S(2)}, u32[]{:S(2)}) async-start(f32[64,1,24]{2,1,0:T(1,128)} %tile.2), calls=%async_computation | async-start | bytes 65536 | tf_op jit(solution)/shard_map/all_to_all | solution.py:15
  446.7 21.6 %while.1 = (s32[]{:T(128)}, f32[768,768]{0,1:T(8,128)}, s32[6,2]{0,1:T(2,128)S(1)}, f32[6,128,128]{2,1,0:T(8,128)}, s32[]{:T(128)}) while((s32[]{:T(128)}, f32[768,768]{0,1:T(8,128)}, s32[6,2]{0,1:T(2,128)S(1)}, f32[6,128,128]{2,1,0:T(8,128)}, s32[]{:T(128)}) %tuple.82), condition=%wide.while_cond, body=%wide.while_body.sunk | while | flops 2 | bytes 393329 | solution.py:144
  468.4 59.8 %custom-call.53 = f32[6,128,128]{1,2,0:T(8,128)S(1)} custom-call(f32[6,128,128]{2,1,0:T(8,128)} %get-tuple-element.10), custom_call_target="InvertDiagBlocksLowerTriangular" | custom-call | tf_op jit(solution)/shard_map/triangular_solve | solution.py:144
  (233 shorter events, 129.0 us)
Async XLA Ops:
  7.2 15.0 %copy-start = (f32[2,768]{1,0:T(2,128)S(1)}, f32[2,768]{1,0:T(2,128)}, u32[]{:S(2)}) copy-start(f32[2,768]{1,0:T(2,128)} %param.11) | copy-start | bytes 18436
  7.2 35.5 %all-gather.2.cloned.1.call-start = ((), (), s32[]{:S(2)}) async-start(), calls=%async_computation.1 | async-start | bytes 1966080 | tf_op jit(solution)/shard_map/all_gather | solution.py:182
  42.7 22.0 %collective-permute-start = (bf16[2,48,64,128]{3,2,1,0:T(8,128)(2,1)}, bf16[2,48,64,128]{3,2,1,0:T(8,128)(2,1)S(1)}, u32[]{:S(2)}, u32[]{:S(2)}) collective-permute-start(bf16[2,48,64,128]{3,2,1,0:T(8,128)(2,1)} %all-gather.2.cloned.1.call-done), channel_id=1, source_target_pairs={{4,0},{8,4},{12,8},{16,12},{20,16},{24,20},{28,24},{32,28},{36,32}... | collective-permute-start | bytes 4718600 | tf_op jit(solution)/shard_map/ppermute | solution.py:23
  51.2 15.3 %copy-start.4 = (bf16[2,12,64,128]{3,2,1,0:T(8,128)(2,1)S(1)}, bf16[2,12,64,128]{3,2,1,0:T(8,128)(2,1)}, u32[]{:S(2)}) copy-start(bf16[2,12,64,128]{3,2,1,0:T(8,128)(2,1)} %param.9) | copy-start | bytes 1179652
  85.7 2.1 copy-start.2
  85.7 7.5 %copy-start.5 = (bf16[9,256,256]{2,1,0:T(8,128)(2,1)S(1)}, bf16[9,256,256]{2,1,0:T(8,128)(2,1)}, u32[]{:S(2)}) copy-start(bf16[9,256,256]{2,1,0:T(8,128)(2,1)} %param.15) | copy-start | bytes 3538948
  87.9 7.6 %collective-permute-start.2 = (bf16[4,1,64,256]{3,2,1,0:T(8,128)(2,1)S(1)}, bf16[4,1,64,256]{3,2,1,0:T(8,128)(2,1)S(1)}, u32[]{:S(2)}, u32[]{:S(2)}) collective-permute-start(bf16[4,1,64,256]{3,2,1,0:T(8,128)(2,1)S(1)} %get-tuple-element.45), channel_id=1, source_target_pairs={{1,0},{2,1},{3,2},{5,4},{6,5},{7,6},{9,8},{10,9},{11,10},{13,12},{... | collective-permute-start | bytes 393224 | tf_op jit(solution)/shard_map/ppermute | solution.py:36
  89.2 6.3 %collective-permute-start.1 = (bf16[4,1,64,256]{3,2,1,0:T(8,128)(2,1)S(1)}, bf16[4,1,64,256]{3,2,1,0:T(8,128)(2,1)S(1)}, u32[]{:S(2)}, u32[]{:S(2)}) collective-permute-start(bf16[4,1,64,256]{3,2,1,0:T(8,128)(2,1)S(1)} %get-tuple-element.44), channel_id=1, source_target_pairs={{0,1},{1,2},{2,3},{4,5},{5,6},{6,7},{8,9},{9,10},{10,11},{12,13},{... | collective-permute-start | bytes 393224 | tf_op jit(solution)/shard_map/ppermute | solution.py:34
  108.4 6.0 %collective-permute-start.4 = (bf16[4,1,64,128]{3,2,1,0:T(8,128)(2,1)S(1)}, bf16[4,1,64,128]{3,2,1,0:T(8,128)(2,1)S(1)}, u32[]{:S(2)}, u32[]{:S(2)}) collective-permute-start(bf16[4,1,64,128]{3,2,1,0:T(8,128)(2,1)S(1)} %get-tuple-element.49), channel_id=1, source_target_pairs={{1,0},{2,1},{3,2},{5,4},{6,5},{7,6},{9,8},{10,9},{11,10},{13,12},{... | collective-permute-start | bytes 196616 | tf_op jit(solution)/shard_map/ppermute | solution.py:36
  109.7 5.4 collective-permute-start.3
  114.2 1.2 copy-start.6
  120.0 2.3 copy-start.7
  295.6 1.4 copy-start.3
  434.8 93.3 %all-to-all-start = ((f32[64,1,24]{2,1,0:T(1,128)}), f32[64,1,24]{2,1,0:T(1,128)S(1)}, u32[]{:S(2)}, u32[]{:S(2)}) async-start(f32[64,1,24]{2,1,0:T(1,128)} %tile.2), calls=%async_computation | async-start | bytes 65536 | tf_op jit(solution)/shard_map/all_to_all | solution.py:15
  446.7 97.6 %copy-start.1 = (f32[2,768]{1,0:T(2,128)S(1)}, f32[2,768]{1,0:T(2,128)}, u32[]{:S(2)}) copy-start(f32[2,768]{1,0:T(2,128)} %param.11) | copy-start | bytes 18436
Sparse Core Ops, SparseCore 0:
  9.8 32.8 all-gather.1
